TPU v7x, 32 devices: a whole 2x2x4 slice. The times are simulated.
32 devices in a mesh: row: 4 (over y, x), dict: 8 (over z, core).
Axes of the slice: x: 2, y: 2, z: 4, core: 2. Of those that a mesh axis runs over, the one named last changes fastest.
Arguments:
- activations: bfloat16 [4096, 4096], P(('row', 'dict')), may hold values from -6 to 6
- block_ids: int32 [4096, 4], P(('row', 'dict')), may hold values from 0 to 15, all different within a row; in each aligned block of 128 rows (0 to 127, 128 to 255, ...) at most 48 rows name the same one
- enc_weight: bfloat16 [2048, 4096], P('dict'), may hold values from -0.09375 to 0.09375
- enc_bias: float32 [2048], P('dict'), may hold values from -3 to 3
- dec_weight: bfloat16 [2048, 4096], P('dict'), may hold values from -0.25 to 0.25
- dec_bias: float32 [4096], replicated, may hold values from -3 to 3
Outputs:
- rebuilt: bfloat16 [4096, 4096], P(('row', 'dict'))
- enc_grad: bfloat16 [4096, 2048], P('row', 'dict')
- dec_grad: bfloat16 [4096, 2048], P('row', 'dict')
Inputs may be any that keep to these rules, and one draw needn't show every extreme that they name: `block_ids`: each row names 4 different blocks. Among the rows of one device no block is named by more than 48 rows, and some block is named by exactly 48.
All inputs are finite; a program needn't handle non-finite values.
Results may differ from a plain program's by a relative error of at most 0.0059.
Values may be sent and summed in bfloat16 or wider, within the bound.
A program may use at most 128 MiB of HBM per device.

v0:
```python
import jax
import jax.numpy as jnp
from jax import lax
from jax.sharding import PartitionSpec as P

BS = 128
K = 4
LOSS_SCALE = 0.03125


def gelu_tanh(values):
    return jax.nn.gelu(values, approximate=True)


def gelu_grad(pre_act, upstream):
    return jax.vjp(gelu_tanh, pre_act)[1](upstream)[0]


def slot_plan(block_ids, groups, total_blocks, slot_depth):
    rows_total = block_ids.shape[0]
    picks = block_ids.shape[1]
    per_group = rows_total // groups
    flat_ids = block_ids.reshape(groups, per_group * picks)
    onehot = (
        flat_ids[:, :, None] == jnp.arange(total_blocks, dtype=jnp.int32)[None, None, :]
    ).astype(jnp.int32)
    rank_in_block = jnp.sum((jnp.cumsum(onehot, axis=1) - 1) * onehot, axis=2)
    group_index = jnp.arange(groups, dtype=jnp.int32)[:, None]
    target = ((flat_ids * groups + group_index) * slot_depth + rank_in_block).reshape(-1)
    source_row = jnp.arange(rows_total * picks, dtype=jnp.int32) // picks
    filled = (
        jnp.full((total_blocks * groups * slot_depth,), rows_total, jnp.int32)
        .at[target]
        .set(source_row)
    )
    return (target, filled)


def pack_rows(values, filled, shape):
    padded = jnp.concatenate([values, jnp.zeros((1, values.shape[1]), values.dtype)], axis=0)
    return padded[filled].reshape(shape)


def on_device(activations, block_ids, enc_weight, enc_bias, dec_weight, dec_bias):
    rows_here, features = activations.shape
    dict_size = lax.axis_size("dict")
    row_size = lax.axis_size("row")
    local_latents = enc_weight.shape[0]
    block_count = local_latents // BS
    total_blocks = block_count * dict_size
    slot_depth = max(2, 3 * rows_here * K // (2 * total_blocks))
    enc_blocks = enc_weight.reshape(block_count, BS, features)
    dec_blocks = dec_weight.reshape(block_count, BS, features)
    bias_blocks = enc_bias.reshape(block_count, BS)
    shifted = (activations.astype(jnp.float32) - dec_bias[None, :]).astype(jnp.bfloat16)
    target, filled = slot_plan(block_ids, 1, total_blocks, slot_depth)
    outgoing = pack_rows(shifted, filled, (dict_size, block_count, slot_depth, features))
    encode_received = lax.all_to_all(outgoing, "dict", split_axis=0, concat_axis=0, tiled=True)
    pre_act = jnp.einsum(
        "sbmd,bcd->sbmc", encode_received, enc_blocks, preferred_element_type=jnp.float32
    )
    pre_act = pre_act + bias_blocks[None, :, None, :]
    encode_latent = gelu_tanh(pre_act).astype(jnp.bfloat16)
    partial_value = jnp.einsum(
        "sbmc,bcd->sbmd", encode_latent, dec_blocks, preferred_element_type=jnp.float32
    ).astype(jnp.bfloat16)
    partial_value, pre_act, latent, received = (
        partial_value,
        pre_act,
        encode_latent,
        encode_received,
    )
    returned = lax.all_to_all(partial_value, "dict", split_axis=0, concat_axis=0, tiled=True)
    slot_parts = (
        returned.reshape(-1, features)[target].astype(jnp.float32).reshape(rows_here, K, features)
    )
    recon_full = dec_bias[None, :] + jnp.sum(slot_parts, axis=1)
    rebuilt = recon_full.astype(jnp.bfloat16)
    residual = ((recon_full - activations.astype(jnp.float32)) * LOSS_SCALE).astype(jnp.bfloat16)
    residual_sent = pack_rows(residual, filled, (dict_size, block_count, slot_depth, features))
    residual_held = lax.all_to_all(residual_sent, "dict", split_axis=0, concat_axis=0, tiled=True)
    upstream = jnp.einsum(
        "sbmd,bcd->sbmc", residual_held, dec_blocks, preferred_element_type=jnp.float32
    )
    latent_grad = gelu_grad(pre_act, upstream).astype(jnp.bfloat16)
    product = jnp.einsum(
        "sbmc,sbmd->dbc", latent, residual_held, preferred_element_type=jnp.float32
    )
    dec_grad = lax.psum_scatter(
        product.reshape(features // row_size * lax.axis_size("row"), local_latents),
        "row",
        scatter_dimension=0,
        tiled=True,
    ).astype(jnp.bfloat16)
    product = jnp.einsum(
        "sbmc,sbmd->dbc", latent_grad, received, preferred_element_type=jnp.float32
    )
    enc_grad = lax.psum_scatter(
        product.reshape(features // row_size * lax.axis_size("row"), local_latents),
        "row",
        scatter_dimension=0,
        tiled=True,
    ).astype(jnp.bfloat16)
    return (rebuilt, enc_grad, dec_grad)


def gelu_and_slope(values):
    inner = 0.7978845608 * (values + 0.044715 * values * values * values)
    bend = jnp.tanh(inner)
    half = 0.5 * (1.0 + bend)
    slope = half + 0.5 * values * (1.0 - bend * bend) * 0.7978845608 * (
        1.0 + 3.0 * 0.044715 * values * values
    )
    return (values * half, slope)


def dense_on_device(activations, block_ids, enc_weight, enc_bias, dec_weight, dec_bias):
    local_latents = enc_weight.shape[0]
    block_count = local_latents // BS
    me = lax.axis_index("dict")
    shifted = (activations.astype(jnp.float32) - dec_bias[None, :]).astype(jnp.bfloat16)
    ids = lax.all_gather(block_ids, "dict", axis=0, tiled=True)
    held = lax.all_gather(shifted, "dict", axis=0, tiled=True)
    mine = me * block_count + jnp.arange(local_latents, dtype=jnp.int32) // BS
    mask = jnp.any(ids[:, :, None] == mine[None, None, :], axis=1)
    pre_act = lax.dot_general(
        held, enc_weight, (((1,), (1,)), ((), ())), preferred_element_type=jnp.float32
    )
    pre_act = pre_act + enc_bias[None, :]
    value, slope = gelu_and_slope(pre_act)
    latent = jnp.where(mask, value, 0.0).astype(jnp.bfloat16)
    slope = jnp.where(mask, slope, 0.0)
    partial_sum = jnp.dot(latent, dec_weight, preferred_element_type=jnp.float32)
    total = lax.psum_scatter(
        partial_sum.astype(jnp.bfloat16), "dict", scatter_dimension=0, tiled=True
    )
    recon_full = dec_bias[None, :] + total.astype(jnp.float32)
    rebuilt = recon_full.astype(jnp.bfloat16)
    residual = ((recon_full - activations.astype(jnp.float32)) * LOSS_SCALE).astype(jnp.bfloat16)
    residual_held = lax.all_gather(residual, "dict", axis=0, tiled=True)
    upstream = lax.dot_general(
        residual_held, dec_weight, (((1,), (1,)), ((), ())), preferred_element_type=jnp.float32
    )
    latent_grad = (slope * upstream).astype(jnp.bfloat16)

    def reduced(rows_by_features, rows_by_latents):
        product = lax.dot_general(
            rows_by_features,
            rows_by_latents,
            (((0,), (0,)), ((), ())),
            preferred_element_type=jnp.float32,
        )
        return lax.psum_scatter(product, "row", scatter_dimension=0, tiled=True).astype(
            jnp.bfloat16
        )

    dec_grad = reduced(residual_held, latent)
    enc_grad = reduced(held, latent_grad)
    return (rebuilt, enc_grad, dec_grad)


def solution(mesh):
    few_blocks = mesh.shape["dict"] <= 8
    return jax.shard_map(
        dense_on_device if few_blocks else on_device,
        mesh=mesh,
        in_specs=(
            P(("row", "dict"), None),
            P(("row", "dict"), None),
            P("dict", None),
            P("dict"),
            P("dict", None),
            P(),
        ),
        out_specs=(P(("row", "dict"), None), P("row", "dict"), P("row", "dict")),
        check_vma=False,
    )
```

profile of v0, /device:TPU:0, one launch (start us, length us, event | category | flops | bytes accessed | tf_op | source)
XLA Modules:
  0.0 404.1 jit_solution(12838851521415117076)
XLA Ops:
  7.2 0.0 copy-start
  7.2 0.0 all-gather.3.cloned.1.call-start
  7.2 2.5 fusion
  9.8 0.0 all-gather.3.cloned.1.call-update
  9.8 0.0 reduce-scatter.4.cloned.1.call-start
  9.8 14.5 %all_gather.9 = s32[1024,4]{0,1:T(4,128)S(1)} all-gather(s32[128,4]{0,1:T(4,128)} %param.7), channel_id=1, replica_groups=mesh['row'=4,'dict'=8] {'dict'}, dimensions={0}, use_global_device_ids=true | all-gather | bytes 18432 | tf_op jit(solution)/shard_map/all_gather | solution.py:122
  24.4 1.0 compare_reduce_fusion
  25.4 69.6 %all-gather.3.cloned.1.call-done = bf16[1024,4096]{1,0:T(8,128)(2,1)} async-done(((bf16[128,4096]{1,0:T(8,128)(2,1)}), bf16[1024,4096]{1,0:T(8,128)(2,1)}) %all-gather.3.cloned.1.call-update) | async-done | bytes 8388624 | tf_op jit(solution)/shard_map/all_gather | solution.py:123
  95.0 6.4 %convolution_add_fusion = f32[1024,256]{1,0:T(8,128)S(1)} fusion(bf16[1024,4096]{1,0:T(8,128)(2,1)} %all-gather.3.cloned.1.call-done, bf16[256,4096]{1,0:T(8,128)(2,1)} %param.8, f32[256]{0:T(256)} %param.9), kind=kOutput, calls=%fused_computation.12 | convolution fusion | flops 2147745792 | bytes 11535360 | tf_op jit(solution)/shard_map/dot_general | solution.py:126
  101.4 0.0 copy-start.2
  101.4 1.0 copy-done.2
  102.3 0.0 copy-done
  102.3 5.8 %convolution_convert_fusion = bf16[1024,4096]{1,0:T(8,128)(2,1)} fusion(bf16[256,4096]{1,0:T(8,128)(2,1)S(1)} %copy-done, pred[1024,256]{1,0:T(8,128)(4,1)S(1)} %compare_reduce_fusion, f32[1024,256]{1,0:T(8,128)S(1)} %convolution_add_fusion), kind=kOutput, calls=%fused_computation | convolution fusion | flops 2154299392 | bytes 11796480 | tf_op jit(solution)/shard_map/dot_general | solution.py:133
  108.1 0.0 reduce-scatter.4.cloned.1.call-update
  108.1 0.0 all-gather.5.cloned.1.call-start
  108.2 88.3 %reduce-scatter.4.cloned.1.call-done = bf16[128,4096]{1,0:T(8,128)(2,1)} async-done(((bf16[1024,4096]{1,0:T(8,128)(2,1)}), bf16[128,4096]{1,0:T(8,128)(2,1)}) %reduce-scatter.4.cloned.1.call-update) | async-done | bytes 1048592 | tf_op jit(solution)/shard_map/reduce_scatter | solution.py:134
  196.4 0.0 copy-done.1
  196.4 0.0 copy-done.4
  196.4 3.0 fusion.2
  199.5 0.0 all-gather.5.cloned.1.call-update
  199.5 0.0 reduce-scatter.8.cloned.1.call-start
  199.5 80.5 %all-gather.5.cloned.1.call-done = bf16[1024,4096]{1,0:T(8,128)(2,1)} async-done(((bf16[128,4096]{1,0:T(8,128)(2,1)}), bf16[1024,4096]{1,0:T(8,128)(2,1)}) %all-gather.5.cloned.1.call-update) | async-done | bytes 8388624 | tf_op jit(solution)/shard_map/all_gather | solution.py:140
  280.1 8.2 %fusion.12 = f32[4096,256]{1,0:T(8,128)} fusion(bf16[1024,4096]{1,0:T(8,128)(2,1)} %all-gather.5.cloned.1.call-done, pred[1024,256]{1,0:T(8,128)(4,1)S(1)} %compare_reduce_fusion, f32[1024,256]{1,0:T(8,128)} %copy-done.2), kind=kOutput, calls=%fused_computation.27 | convolution fusion | flops 2150105088 | bytes 13893632 | tf_op jit(solution)/shard_map/dot_general | solution.py:147
  288.2 0.0 reduce-scatter.8.cloned.1.call-update
  288.3 0.2 reduce-scatter.6.cloned.1.call-start
  288.5 1.0 copy-done.3
  289.5 17.6 %fusion.13 = f32[4096,256]{1,0:T(8,128)} fusion(bf16[1024,4096]{1,0:T(8,128)(2,1)} %all-gather.3.cloned.1.call-done, bf16[1024,4096]{1,0:T(8,128)(2,1)} %all-gather.5.cloned.1.call-done, bf16[256,4096]{1,0:T(8,128)(2,1)S(1)} %copy-done, pred[1024,256]{1,0:T(8,128)(4,1)S(1)} %compare_reduce_fusion, f32[1024,256]{1,0:T(8,128)S(1)} %copy-done.3), kind=kOutput, calls=%fused_computation.28 | convolution fusion | flops 4300210176 | bytes 24379392 | tf_op jit(solution)/shard_map/dot_general | solution.py:147
  307.1 0.0 reduce-scatter.6.cloned.1.call-update
  307.1 32.5 %reduce-scatter.8.cloned.1.call-done = f32[1024,256]{1,0:T(8,128)} async-done(((f32[4096,256]{1,0:T(8,128)}), f32[1024,256]{1,0:T(8,128)}) %reduce-scatter.8.cloned.1.call-update) | async-done | bytes 1048592 | tf_op jit(solution)/shard_map/reduce_scatter | solution.py:153
  339.6 2.1 convert_element_type.40
  341.7 53.8 %reduce-scatter.6.cloned.1.call-done = f32[1024,256]{1,0:T(8,128)} async-done(((f32[4096,256]{1,0:T(8,128)}), f32[1024,256]{1,0:T(8,128)}) %reduce-scatter.6.cloned.1.call-update) | async-done | bytes 1048592 | tf_op jit(solution)/shard_map/reduce_scatter | solution.py:153
  395.5 2.1 convert_element_type.39
  (4 shorter events, 0.0 us)
Async XLA Ops:
  7.2 95.2 %copy-start = (bf16[256,4096]{1,0:T(8,128)(2,1)S(1)}, bf16[256,4096]{1,0:T(8,128)(2,1)}, u32[]{:S(2)}) copy-start(bf16[256,4096]{1,0:T(8,128)(2,1)} %param.10) | copy-start | bytes 6291460
  7.2 87.8 %all-gather.3.cloned.1.call-start = ((), (), s32[]{:S(2)}) async-start(), calls=%async_computation.3 | async-start | bytes 9437184 | tf_op jit(solution)/shard_map/all_gather | solution.py:123
  9.8 186.6 %reduce-scatter.4.cloned.1.call-start = ((), (), s32[]{:S(2)}) async-start(), calls=%async_computation.4 | async-start | bytes 9437184 | tf_op jit(solution)/shard_map/reduce_scatter | solution.py:134
  101.4 1.0 copy-start.2
  108.1 88.3 %copy-start.1 = (bf16[128,4096]{1,0:T(8,128)(2,1)S(1)}, bf16[128,4096]{1,0:T(8,128)(2,1)}, u32[]{:S(2)}) copy-start(bf16[128,4096]{1,0:T(8,128)(2,1)} %param.6) | copy-start | bytes 3145732
  108.1 88.3 %copy-start.4 = (f32[4096]{0:T(1024)S(1)}, f32[4096]{0:T(1024)}, u32[]{:S(2)}) copy-start(f32[4096]{0:T(1024)} %param.11) | copy-start | bytes 49156
  108.1 171.9 %all-gather.5.cloned.1.call-start = ((), (), s32[]{:S(2)}) async-start(), calls=%async_computation.5 | async-start | bytes 9437184 | tf_op jit(solution)/shard_map/all_gather | solution.py:140
  199.5 140.1 %reduce-scatter.8.cloned.1.call-start = ((), (), s32[]{:S(2)}) async-start(), calls=%async_computation.7 | async-start | bytes 5242880 | tf_op jit(solution)/shard_map/reduce_scatter | solution.py:153
  288.2 1.2 copy-start.3
  288.3 107.2 %reduce-scatter.6.cloned.1.call-start = ((), (), s32[]{:S(2)}) async-start(), calls=%async_computation.6 | async-start | bytes 5242880 | tf_op jit(solution)/shard_map/reduce_scatter | solution.py:153
Sparse Core Ops, SparseCore 0:
  10.2 84.7 all-gather.2
  108.2 88.1 reduce-scatter.3
  199.6 80.3 all-gather.4
  288.4 51.2 reduce-scatter.7
  342.7 52.6 reduce-scatter.5
where the time goes:
time: 404 us
  waiting for transfers between devices  325 us (80%)
  matrix products  38 us (9%)
  blocking collectives  14.5 us (4%)
  between operations  13.8 us (3%)
  other arithmetic  10.7 us (3%)
    reduce_scatter x1, waiting for transfers between devices, dense_on_device(): lax.psum_scatter(partial_sum.astype(jnp.bfloat16), 'dict', scatter_dimens...  88.3 us
    reduce_scatter x2, waiting for transfers between devices, reduced(): lax.psum_scatter(product, 'row', scatter_dimension=0, tiled=True)  86.3 us
    all_gather x1, waiting for transfers between devices, dense_on_device(): residual_held = lax.all_gather(residual, 'dict', axis=0, tiled=True)  80.5 us
    all_gather x1, waiting for transfers between devices, dense_on_device(): held = lax.all_gather(shifted, 'dict', axis=0, tiled=True)  69.6 us
    dot_general x2, matrix products, reduced(): lax.dot_general(rows_by_features, rows_by_latents, (((0,), (0,)), ((), ()...  25.8 us
    all_gather x1, blocking collectives, dense_on_device(): ids = lax.all_gather(block_ids, 'dict', axis=0, tiled=True)  14.5 us
  transfers between devices with their start and end apart: 5, of which 5 were waited for; matrix products, arithmetic and copies ran while one was open for 5% of the time, Pallas kernels for 0%

commit v1 on v0

--- a/solution.py
+++ b/solution.py
@@ -2,6 +2,7 @@
 import jax.numpy as jnp
 from jax import lax
 from jax.sharding import PartitionSpec as P
+from jax.lax import all_gather
 
 BS = 128
 K = 4
@@ -119,8 +120,9 @@
     block_count = local_latents // BS
     me = lax.axis_index("dict")
     shifted = (activations.astype(jnp.float32) - dec_bias[None, :]).astype(jnp.bfloat16)
-    ids = lax.all_gather(block_ids, "dict", axis=0, tiled=True)
-    held = lax.all_gather(shifted, "dict", axis=0, tiled=True)
+    view_out = jnp.concatenate([block_ids, shifted], 1)
+    now = all_gather(view_out, axis_name="dict", axis=0, tiled=True)
+    ids, held = jnp.split(now, [block_ids.shape[1]], 1)
     mine = me * block_count + jnp.arange(local_latents, dtype=jnp.int32) // BS
     mask = jnp.any(ids[:, :, None] == mine[None, None, :], axis=1)
     pre_act = lax.dot_general(

time: 404 us -> 411 us (1.017)
  waiting for transfers between devices: 325 us -> 342 us
  blocking collectives: 14.5 us -> 0 us
    all_gather x1, waiting for transfers between devices: 69.6 us -> 87 us  [dense_on_device(): now = all_gather(view_out, axis_name='dict', axis=0, tiled=True)]
    all_gather x1 -> x0, blocking collectives: 14.5 us -> none  [dense_on_device(): ids = lax.all_gather(block_ids, 'dict', axis=0, tiled=True)]
where the time goes in v1:
time: 411 us; the launch traced here: 410 us
  waiting for transfers between devices  342 us (83%)
  matrix products  39.2 us (10%)
  between operations  13.9 us (3%)
  other arithmetic  11.7 us (3%)
    reduce_scatter x1, waiting for transfers between devices, dense_on_device(): lax.psum_scatter(partial_sum.astype(jnp.bfloat16), 'dict', scatter_dimens...  88.2 us
    all_gather x1, waiting for transfers between devices, dense_on_device(): now = all_gather(view_out, axis_name='dict', axis=0, tiled=True)  87 us
    reduce_scatter x2, waiting for transfers between devices, reduced(): lax.psum_scatter(product, 'row', scatter_dimension=0, tiled=True)  86.1 us
    all_gather x1, waiting for transfers between devices, dense_on_device(): residual_held = lax.all_gather(residual, 'dict', axis=0, tiled=True)  80.5 us
    dot_general x2, matrix products, reduced(): lax.dot_general(rows_by_features, rows_by_latents, (((0,), (0,)), ((), ()...  25.9 us
  transfers between devices with their start and end apart: 5, of which 5 were waited for; matrix products, arithmetic and copies ran while one was open for 5% of the time, Pallas kernels for 0%

profile of v1, /device:TPU:0, one launch (start us, length us, event | category | flops | bytes accessed | tf_op | source)
XLA Modules:
  0.0 410.3 jit_solution(8900284311634450629)
XLA Ops:
  7.2 0.0 copy-start
  7.2 0.0 all-gather.3.cloned.1.call-start
  7.2 0.8 convert_element_type.42
  8.1 0.1 copy.10
  8.2 1.4 fusion.4
  9.6 1.5 pad_maximum_fusion
  11.1 0.0 all-gather.3.cloned.1.call-update
  11.1 0.0 reduce-scatter.4.cloned.1.call-start
  11.2 87.0 %all-gather.3.cloned.1.call-done = bf16[1024,4100]{1,0:T(8,128)(2,1)} async-done(((bf16[128,4100]{1,0:T(8,128)(2,1)}), bf16[1024,4100]{1,0:T(8,128)(2,1)}) %all-gather.3.cloned.1.call-update) | async-done | bytes 8396816 | tf_op jit(solution)/shard_map/all_gather | solution.py:124
  98.2 1.0 split.8
  99.2 0.1 copy.11
  99.3 0.9 compare_reduce_fusion
  100.2 7.5 %fusion.8 = f32[1024,256]{1,0:T(8,128)S(1)} fusion(bf16[256,4096]{1,0:T(8,128)(2,1)} %param.8, bf16[1024,4100]{1,0:T(8,128)(2,1)} %all-gather.3.cloned.1.call-done, f32[256]{0:T(256)S(1)} %copy-done.5), kind=kOutput, calls=%fused_computation.16 | convolution fusion | flops 2147745792 | bytes 11535360 | tf_op jit(solution)/shard_map/dot_general | solution.py:128
  107.7 1.0 copy-done.2
  108.7 5.7 %convolution_convert_fusion = bf16[1024,4096]{1,0:T(8,128)(2,1)} fusion(bf16[256,4096]{1,0:T(8,128)(2,1)S(1)} %copy-done, pred[1024,256]{1,0:T(8,128)(4,1)S(1)} %compare_reduce_fusion, f32[1024,256]{1,0:T(8,128)S(1)} %fusion.8), kind=kOutput, calls=%fused_computation | convolution fusion | flops 2154299392 | bytes 11796480 | tf_op jit(solution)/shard_map/dot_general | solution.py:135
  114.5 0.0 reduce-scatter.4.cloned.1.call-update
  114.5 0.0 all-gather.5.cloned.1.call-start
  114.5 88.2 %reduce-scatter.4.cloned.1.call-done = bf16[128,4096]{1,0:T(8,128)(2,1)} async-done(((bf16[1024,4096]{1,0:T(8,128)(2,1)}), bf16[128,4096]{1,0:T(8,128)(2,1)}) %reduce-scatter.4.cloned.1.call-update) | async-done | bytes 1048592 | tf_op jit(solution)/shard_map/reduce_scatter | solution.py:136
  202.8 3.0 fusion.6
  205.8 0.0 all-gather.5.cloned.1.call-update
  205.8 0.0 reduce-scatter.8.cloned.1.call-start
  205.8 80.5 %all-gather.5.cloned.1.call-done = bf16[1024,4096]{1,0:T(8,128)(2,1)} async-done(((bf16[128,4096]{1,0:T(8,128)(2,1)}), bf16[1024,4096]{1,0:T(8,128)(2,1)}) %all-gather.5.cloned.1.call-update) | async-done | bytes 8388624 | tf_op jit(solution)/shard_map/all_gather | solution.py:142
  286.3 8.2 %fusion.20 = f32[4096,256]{1,0:T(8,128)} fusion(bf16[1024,4096]{1,0:T(8,128)(2,1)} %all-gather.5.cloned.1.call-done, pred[1024,256]{1,0:T(8,128)(4,1)S(1)} %compare_reduce_fusion, f32[1024,256]{1,0:T(8,128)} %copy-done.2), kind=kOutput, calls=%fused_computation.33 | convolution fusion | flops 2150105088 | bytes 13893632 | tf_op jit(solution)/shard_map/dot_general | solution.py:149
  294.5 0.0 reduce-scatter.8.cloned.1.call-update
  294.5 0.2 reduce-scatter.6.cloned.1.call-start
  294.8 1.0 copy-done.3
  295.7 17.8 %fusion = f32[4096,256]{1,0:T(8,128)} fusion(bf16[1024,4100]{1,0:T(8,128)(2,1)} %all-gather.3.cloned.1.call-done, bf16[1024,4096]{1,0:T(8,128)(2,1)} %all-gather.5.cloned.1.call-done, bf16[256,4096]{1,0:T(8,128)(2,1)S(1)} %copy-done, pred[1024,256]{1,0:T(8,128)(4,1)S(1)} %compare_reduce_fusion, f32[1024,256]{1,0:T(8,128)S(1)} %copy-done.3), kind=kOutput, calls=%fused_computation.1 | convolution fusion | flops 4300210176 | bytes 24379392 | tf_op jit(solution)/shard_map/dot_general | solution.py:149
  313.5 0.0 reduce-scatter.6.cloned.1.call-update
  313.5 32.4 %reduce-scatter.8.cloned.1.call-done = f32[1024,256]{1,0:T(8,128)} async-done(((f32[4096,256]{1,0:T(8,128)}), f32[1024,256]{1,0:T(8,128)}) %reduce-scatter.8.cloned.1.call-update) | async-done | bytes 1048592 | tf_op jit(solution)/shard_map/reduce_scatter | solution.py:155
  345.9 2.1 convert_element_type.53
  348.0 53.8 %reduce-scatter.6.cloned.1.call-done = f32[1024,256]{1,0:T(8,128)} async-done(((f32[4096,256]{1,0:T(8,128)}), f32[1024,256]{1,0:T(8,128)}) %reduce-scatter.6.cloned.1.call-update) | async-done | bytes 1048592 | tf_op jit(solution)/shard_map/reduce_scatter | solution.py:155
  401.7 2.1 convert_element_type.52
  (10 shorter events, 0.0 us)
Async XLA Ops:
  7.2 101.6 %copy-start = (bf16[256,4096]{1,0:T(8,128)(2,1)S(1)}, bf16[256,4096]{1,0:T(8,128)(2,1)}, u32[]{:S(2)}) copy-start(bf16[256,4096]{1,0:T(8,128)(2,1)} %param.10) | copy-start | bytes 6291460
  7.2 91.0 %all-gather.3.cloned.1.call-start = ((), (), s32[]{:S(2)}) async-start(), calls=%async_computation.3 | async-start | bytes 9732096 | tf_op jit(solution)/shard_map/all_gather | solution.py:124
  9.6 90.6 %copy-start.5 = (f32[256]{0:T(256)S(1)}, f32[256]{0:T(256)}, u32[]{:S(2)}) copy-start(f32[256]{0:T(256)} %param.9) | copy-start | bytes 3076
  11.1 191.7 %reduce-scatter.4.cloned.1.call-start = ((), (), s32[]{:S(2)}) async-start(), calls=%async_computation.4 | async-start | bytes 9437184 | tf_op jit(solution)/shard_map/reduce_scatter | solution.py:136
  107.7 1.0 copy-start.2
  114.5 88.3 %copy-start.1 = (bf16[128,4096]{1,0:T(8,128)(2,1)S(1)}, bf16[128,4096]{1,0:T(8,128)(2,1)}, u32[]{:S(2)}) copy-start(bf16[128,4096]{1,0:T(8,128)(2,1)} %param.6) | copy-start | bytes 3145732
  114.5 88.3 %copy-start.4 = (f32[4096]{0:T(1024)S(1)}, f32[4096]{0:T(1024)}, u32[]{:S(2)}) copy-start(f32[4096]{0:T(1024)} %param.11) | copy-start | bytes 49156
  114.5 171.8 %all-gather.5.cloned.1.call-start = ((), (), s32[]{:S(2)}) async-start(), calls=%async_computation.5 | async-start | bytes 9437184 | tf_op jit(solution)/shard_map/all_gather | solution.py:142
  205.8 140.1 %reduce-scatter.8.cloned.1.call-start = ((), (), s32[]{:S(2)}) async-start(), calls=%async_computation.7 | async-start | bytes 5242880 | tf_op jit(solution)/shard_map/reduce_scatter | solution.py:155
  294.5 1.2 copy-start.3
  294.5 107.2 %reduce-scatter.6.cloned.1.call-start = ((), (), s32[]{:S(2)}) async-start(), calls=%async_computation.6 | async-start | bytes 5242880 | tf_op jit(solution)/shard_map/reduce_scatter | solution.py:155
Sparse Core Ops, SparseCore 0:
  11.2 86.9 all-gather.2
  114.6 88.1 reduce-scatter.3
  205.9 80.3 all-gather.4
  294.7 51.2 reduce-scatter.7
  349.0 52.6 reduce-scatter.5
